TPU v7x, 32 devices: a whole 2x2x4 slice. The times are simulated.
32 devices in a mesh: rep: 2 (over y), ctx: 4 (over z), head: 2 (over x), sub: 2 (over core).
Axes of the slice: x: 2, y: 2, z: 4, core: 2. Of those that a mesh axis runs over, the one named last changes fastest.
Arguments:
- hidden_states: bfloat16 [2048, 4096], P(('rep', 'ctx'), ('head', 'sub')), parts along dimension 0, may hold values from -8 to 8
- w_query: bfloat16 [4096, 2048], P('ctx', ('head', 'sub')), may hold values from -0.09375 to 0.09375
- w_key: bfloat16 [4096, 2048], P('ctx', ('head', 'sub')), may hold values from -0.09375 to 0.09375
- w_value: bfloat16 [4096, 2048], P('ctx', ('head', 'sub')), may hold values from -0.09375 to 0.09375
- a_query: bfloat16 [4096, 8], replicated, may hold values from -0.09375 to 0.09375
- a_value: bfloat16 [4096, 8], replicated, may hold values from -0.09375 to 0.09375
- b_query: bfloat16 [8, 2048], P(None, ('head', 'sub')), may hold values from -0.29882812 to 0.29882812
- b_value: bfloat16 [8, 2048], P(None, ('head', 'sub')), may hold values from -0.29882812 to 0.29882812
- positions: int32 [2048], P(('rep', 'ctx')), parts along dimension 0, may hold values from 0 to 99999, as said below
- out_grad: bfloat16 [2048, 2048], P(('rep', 'ctx'), ('head', 'sub')), parts along dimension 0, may hold values from -0.119628906 to 0.119628906
Outputs:
- attn_out: bfloat16 [2048, 2048], P(('rep', 'ctx'), ('head', 'sub')), parts along dimension 0
- grad_a_query: float32 [4096, 16], P(None, 'rep'), parts along dimension 1
- grad_b_query: float32 [16, 2048], P('rep', ('head', 'sub')), parts along dimension 0
- grad_a_value: float32 [4096, 16], P(None, 'rep'), parts along dimension 1
- grad_b_value: float32 [16, 2048], P('rep', ('head', 'sub')), parts along dimension 0
There are 2 independent parts, one for each index of `rep`. A program takes and returns all parts, laid end to end along the dimension named above; an argument that names none is the same for every part. Nothing has to cross between parts.
Inputs may be any that keep to these rules, and one draw needn't show every extreme that they name: `positions`: strictly increasing along the sequence; the first is 0 and the last is 99999.
All inputs are finite; a program needn't handle non-finite values.
Results may differ from a plain program's by a relative error of at most 0.012.
Values may be sent and summed in bfloat16 or wider, within the bound.
A program may use at most 64 MiB of HBM per device.

v0:
```python
import math

import jax
import jax.numpy as jnp
from jax import lax
from jax.sharding import PartitionSpec as P

HEAD_DIM = 128
HEADS = 16
TRAIN_CTX = 4096
MAX_POS = 100000


def passed_along(block, axis, distance):
    devices = range(lax.axis_size(axis))
    route = [((i - distance) % len(devices), i) for i in devices]
    return lax.ppermute(block, axis, route)


def rope_tables(positions):
    half_dim = HEAD_DIM // 2
    inverse = jnp.exp(
        jnp.arange(half_dim, dtype=jnp.float32) * (-2.0 * math.log(10000.0) / HEAD_DIM)
    )
    scaled = positions.astype(jnp.float32) * (TRAIN_CTX / MAX_POS)
    angle = scaled[:, None] * inverse[None, :]
    return (jnp.cos(angle)[:, None, :], jnp.sin(angle)[:, None, :])


def rotate(vectors, cosine, sine):
    half_dim = vectors.shape[-1] // 2
    first = vectors[..., :half_dim]
    second = vectors[..., half_dim:]
    return jnp.concatenate(
        [first * cosine - second * sine, second * cosine + first * sine], axis=-1
    )


def project_back(features, low_grads):
    block_width = min(features.shape[1], 512)
    block_count = features.shape[1] // block_width

    def one_block(number):
        section = lax.dynamic_slice_in_dim(features, number * block_width, block_width, 1).astype(
            jnp.float32
        )
        return lax.dot_general(
            section, low_grads, (((0,), (0,)), ((), ())), precision=lax.Precision.HIGHEST
        )

    blocks = lax.map(one_block, jnp.arange(block_count))
    return blocks.reshape(features.shape[1], low_grads.shape[1])


def local(
    hidden_states, w_query, w_key, w_value, a_query, a_value, b_query, b_value, positions, out_grad
):
    rows_here = hidden_states.shape[0]
    columns = w_query.shape[1]
    heads_here = columns // HEAD_DIM
    rank_cols = a_query.shape[1]
    scale = 1.0 / math.sqrt(HEAD_DIM)
    shard_count = lax.axis_size("ctx")
    total_tokens = rows_here * shard_count
    group_len = total_tokens // 4
    reach = (group_len // 2 % rows_here + group_len - 1) // rows_here
    full_states = lax.all_gather(hidden_states, ("head", "sub"), axis=1, tiled=True)
    pieces = (
        lax.all_gather(w_query, "ctx", axis=0, tiled=True),
        lax.all_gather(w_key, "ctx", axis=0, tiled=True),
        lax.all_gather(w_value, "ctx", axis=0, tiled=True),
    )
    base_q, base_k, base_v = tuple(
        (
            jnp.dot(full_states, weights_piece, preferred_element_type=jnp.float32)
            for weights_piece in pieces
        )
    )
    low_q = jnp.dot(full_states, a_query, preferred_element_type=jnp.float32).astype(jnp.bfloat16)
    low_v = jnp.dot(full_states, a_value, preferred_element_type=jnp.float32).astype(jnp.bfloat16)
    cosine, sine = rope_tables(positions)
    pre_q = base_q + 2.0 * jnp.dot(low_q, b_query, preferred_element_type=jnp.float32)
    queries = rotate(pre_q.reshape(rows_here, heads_here, HEAD_DIM), cosine, sine).astype(
        jnp.bfloat16
    )
    keyed = rotate(base_k.reshape(rows_here, heads_here, HEAD_DIM), cosine, sine).astype(
        jnp.bfloat16
    )
    valued = (base_v + 2.0 * jnp.dot(low_v, b_value, preferred_element_type=jnp.float32)).astype(
        jnp.bfloat16
    )
    valued = valued.reshape(rows_here, heads_here, HEAD_DIM)
    current = jnp.stack([keyed, valued])
    collected = [current]
    for level in range(reach):
        current = passed_along(current, "ctx", 1)
        collected.append(current)
    key_rows = jnp.concatenate([block[0] for block in collected], axis=0)
    value_rows = jnp.concatenate([block[1] for block in collected], axis=0)
    shard_id = lax.axis_index("ctx")
    head_ids = lax.axis_index(("head", "sub")) * heads_here + jnp.arange(heads_here)
    amount = jnp.where(head_ids >= HEADS // 2, group_len // 2, 0).astype(jnp.int32)
    query_pos = shard_id * rows_here + jnp.arange(rows_here, dtype=jnp.int32)
    block_ids = jnp.arange(reach + 1, dtype=jnp.int32)
    source_shard = (shard_id - block_ids) % shard_count
    key_pos = (
        source_shard[:, None] * rows_here + jnp.arange(rows_here, dtype=jnp.int32)[None, :]
    ).reshape(-1)
    query_num = (query_pos[None, :] - amount[:, None]) % total_tokens
    key_num = (key_pos[None, :] - amount[:, None]) % total_tokens
    same_group = key_num[:, None, :] // group_len == query_num[:, :, None] // group_len
    visible = same_group & (key_num[:, None, :] <= query_num[:, :, None])
    scores = (
        jnp.einsum("qhd,khd->hqk", queries, key_rows, preferred_element_type=jnp.float32) * scale
    )
    scores = jnp.where(visible, scores, -jnp.inf)
    highest = jnp.max(scores, axis=-1, keepdims=True)
    expo = jnp.where(visible, jnp.exp(scores - highest), 0.0)
    probs = expo / jnp.sum(expo, axis=-1, keepdims=True)
    probs_b = probs.astype(jnp.bfloat16)
    attended = jnp.einsum("hqk,khd->qhd", probs_b, value_rows, preferred_element_type=jnp.float32)
    attn_out = attended.astype(jnp.bfloat16)
    grads = out_grad.reshape(rows_here, heads_here, HEAD_DIM)
    dprob = jnp.einsum("qhd,khd->hqk", grads, value_rows, preferred_element_type=jnp.float32)
    delta = jnp.sum(grads.astype(jnp.float32) * attn_out.astype(jnp.float32), axis=-1)
    dscore = probs * (dprob - delta.T[:, :, None])
    dscore_b = (dscore * scale).astype(jnp.bfloat16)
    dquery = jnp.einsum("hqk,khd->qhd", dscore_b, key_rows, preferred_element_type=jnp.float32)
    dvalue = jnp.einsum("hqk,qhd->khd", probs_b, grads, preferred_element_type=jnp.float32)
    value_blocks = dvalue.reshape(reach + 1, rows_here, columns)
    carried = value_blocks[reach]
    for level in range(reach, 0, -1):
        carried = passed_along(carried, "ctx", -1) + value_blocks[level - 1]
    dv_local = carried.astype(jnp.bfloat16)
    dq_local = rotate(dquery, cosine, -sine).astype(jnp.bfloat16).reshape(rows_here, columns)
    grad_bq = 2.0 * jnp.dot(low_q.T, dq_local, preferred_element_type=jnp.float32)
    grad_bv = 2.0 * jnp.dot(low_v.T, dv_local, preferred_element_type=jnp.float32)
    low_grads = jnp.concatenate(
        [
            2.0 * jnp.dot(dq_local, b_query.T, preferred_element_type=jnp.float32),
            2.0 * jnp.dot(dv_local, b_value.T, preferred_element_type=jnp.float32),
        ],
        axis=1,
    )
    grad_down = lax.psum(project_back(full_states, low_grads), ("ctx", "head", "sub"))
    grad_bq, grad_bv = lax.psum((grad_bq, grad_bv), "ctx")
    return (
        attn_out.reshape(rows_here, columns),
        grad_down[:, :rank_cols],
        grad_bq,
        grad_down[:, rank_cols:],
        grad_bv,
    )


def solution(mesh):
    in_specs = (
        P(("rep", "ctx"), ("head", "sub")),
        P("ctx", ("head", "sub")),
        P("ctx", ("head", "sub")),
        P("ctx", ("head", "sub")),
        P(),
        P(),
        P(None, ("head", "sub")),
        P(None, ("head", "sub")),
        P(("rep", "ctx")),
        P(("rep", "ctx"), ("head", "sub")),
    )
    out_specs = (
        P(("rep", "ctx"), ("head", "sub")),
        P(None, "rep"),
        P("rep", ("head", "sub")),
        P(None, "rep"),
        P("rep", ("head", "sub")),
    )
    return jax.shard_map(local, mesh=mesh, in_specs=in_specs, out_specs=out_specs, check_vma=False)
```

profile of v0, /device:TPU:0, one launch (start us, length us, event | category | flops | bytes accessed | tf_op | source)
XLA Modules:
  0.0 444.1 jit_solution(10380813642152723503)
XLA Ops:
  7.2 0.7 all-gather.5.cloned.1.call-update
  8.0 0.7 all-gather.9.cloned.1.call-update
  8.7 0.7 all-gather.11.cloned.1.call-update
  9.5 0.5 all-gather.7.cloned.1.call-update
  10.2 1.3 fusion.23
  11.5 23.4 %all-gather.5.cloned.1.call-done = bf16[256,4096]{1,0:T(8,128)(2,1)} async-done(((bf16[256,1024]{1,0:T(8,128)(2,1)}), bf16[256,4096]{1,0:T(8,128)(2,1)}) %all-gather.5.cloned.1.call-update) | async-done | bytes 2097168 | tf_op jit(solution)/shard_map/all_gather | solution.py:67
  34.9 2.4 convolution_convert_fusion.1
  37.3 0.7 convolution_convert_fusion.2
  38.0 79.3 %all-gather.9.cloned.1.call-done = bf16[4096,512]{1,0:T(8,128)(2,1)} async-done(((bf16[1024,512]{1,0:T(8,128)(2,1)}), bf16[4096,512]{1,0:T(8,128)(2,1)}) %all-gather.9.cloned.1.call-update) | async-done | bytes 4194320 | tf_op jit(solution)/shard_map/all_gather | solution.py:70
  117.2 3.4 fusion.50
  120.7 0.2 reshape.368
  120.9 77.2 %all-gather.11.cloned.1.call-done = bf16[4096,512]{1,0:T(8,128)(2,1)} async-done(((bf16[1024,512]{1,0:T(8,128)(2,1)}), bf16[4096,512]{1,0:T(8,128)(2,1)}) %all-gather.11.cloned.1.call-update) | async-done | bytes 4194320 | tf_op jit(solution)/shard_map/all_gather | solution.py:69
  198.1 3.4 fusion.51
  201.5 1.1 fusion.9
  202.6 1.2 reshape.369
  203.8 74.9 %all-gather.7.cloned.1.call-done = bf16[4096,512]{1,0:T(8,128)(2,1)} async-done(((bf16[1024,512]{1,0:T(8,128)(2,1)}), bf16[4096,512]{1,0:T(8,128)(2,1)}) %all-gather.7.cloned.1.call-update) | async-done | bytes 4194320 | tf_op jit(solution)/shard_map/all_gather | solution.py:71
  278.8 3.4 fusion.49
  282.2 0.3 fusion.10
  282.5 0.8 stack_reshape.3
  283.2 1.0 copy.29
  284.3 0.6 fusion.45
  284.9 0.3 copy-done.2
  285.2 1.1 subtract_convert_fusion.1
  286.3 1.0 pad_maximum_fusion
  287.4 1.8 copy.34
  289.2 0.8 copy_bitcast_fusion
  290.0 12.8 %collective-permute-done = bf16[2,256,4,128]{3,1,2,0:T(8,128)(2,1)S(1)} collective-permute-done((bf16[2,256,4,128]{3,1,2,0:T(8,128)(2,1)}, bf16[2,256,4,128]{3,1,2,0:T(8,128)(2,1)S(1)}, u32[]{:S(2)}, u32[]{:S(2)}) %collective-permute-start) | collective-permute-done | bytes 524320 | tf_op jit(solution)/shard_map/ppermute | solution.py:17
  302.8 0.8 slice_bitcast_fusion
  303.6 4.7 %fusion.48 = (f32[4,256]{1,0:T(4,128)S(1)}, f32[4,256,512]{2,1,0:T(8,128)}) fusion(s32[4,256]{1,0:T(4,128)S(1)} %get-tuple-element.79, s32[4,512]{1,0:T(4,128)S(1)} %get-tuple-element.74, s32[4,256]{1,0:T(4,128)S(1)} %get-tuple-element.78, s32[4,512]{1,0:T(4,128)S(1)} %get-tuple-element.73, bf16[256,4,64]{2,0,1:T(8,128)(2,1)} %get-tuple-element.56, ...), kind=kOutput, calls=%fused_computation.106 | convolution fusion | flops 142082560 | bytes 2912256 | tf_op jit(solution)/shard_map/sub | solution.py:118
  308.4 3.1 convolution_bitcast_fusion.1
  311.5 1.3 multiply_reduce_fusion
  312.9 2.6 fusion.7
  315.5 2.2 fusion.44
  317.7 0.3 subtract_convert_fusion
  318.0 0.1 pad_maximum_fusion.7
  318.3 1.8 copy.39
  320.2 0.2 convolution_multiply_fusion.3
  320.4 10.3 %collective-permute-done.1 = f32[256,512]{0,1:T(8,128)} collective-permute-done((f32[256,512]{0,1:T(8,128)}, f32[256,512]{0,1:T(8,128)}, u32[]{:S(2)}, u32[]{:S(2)}) %collective-permute-start.1) | collective-permute-done | bytes 524320 | tf_op jit(solution)/shard_map/ppermute | solution.py:17
  330.7 1.1 fusion.20
  332.0 13.4 %while.10 = (s32[]{:T(128)}, f32[8,512,16]{1,0,2:T(8,128)S(1)}, s32[8]{0:T(128)S(1)}, bf16[256,4096]{1,0:T(8,128)(2,1)S(1)}, f32[256,16]{0,1:T(8,128)S(1)}, /*index=5*/s32[]{:T(128)}, s32[1]{0:T(128)}, s32[]{:T(128)}, s32[]{:T(128)}) while((s32[]{:T(128)}, f32[8,512,16]{1,0,2:T(8,128)S(1)}, s32[8]{0:T(128)S(1)}, ...), condition=%wide.region_4.5_spmd, body=%wide.region_3.4_spmd.sunk | while | flops 25165828 | bytes 442535 | solution.py:51
  332.0 0.6 dynamic_slice.12
  333.2 0.2 convolution_bitcast_fusion.3
  333.5 0.1 dynamic_update_slice.5
  333.6 0.6 dynamic_slice.12
  334.9 0.2 convolution_bitcast_fusion.3
  335.3 0.6 dynamic_slice.12
  336.6 0.2 convolution_bitcast_fusion.3
  336.8 0.1 dynamic_update_slice.5
  337.0 0.6 dynamic_slice.12
  338.2 0.2 convolution_bitcast_fusion.3
  338.7 0.6 dynamic_slice.12
  339.9 0.2 convolution_bitcast_fusion.3
  340.4 0.6 dynamic_slice.12
  341.6 0.2 convolution_bitcast_fusion.3
  342.0 0.6 dynamic_slice.12
  343.3 0.2 convolution_bitcast_fusion.3
  343.7 0.6 dynamic_slice.12
  344.9 0.2 convolution_bitcast_fusion.3
  345.2 0.1 dynamic_update_slice.5
  345.4 0.9 copy.53
  346.3 0.2 convolution_multiply_fusion.2
  346.4 18.4 %all-reduce = (f32[8,512]{1,0:T(8,128)}, f32[8,512]{1,0:T(8,128)}) all-reduce(f32[8,512]{1,0:T(8,128)S(1)} %convolution_multiply_fusion.3, f32[8,512]{1,0:T(8,128)S(1)} %convolution_multiply_fusion.2), channel_id=1, replica_groups=mesh['rep'=2,'ctx'=4,'head'=2,'sub'=2] {'ctx'}, use_global_device_ids=true, to_apply=%region_6.7 | all-reduce | flops 8192 | bytes 65536 | tf_op jit(solution)/shard_map/psum | solution.py:146
  364.8 71.1 %all-reduce.3.cloned.1.call-done = f32[4096,16]{0,1:T(8,128)} async-done(((f32[4096,16]{0,1:T(8,128)}), f32[4096,16]{0,1:T(8,128)}) %all-reduce.3.cloned.1.call-update) | async-done | bytes 262160 | tf_op jit(solution)/shard_map/psum | solution.py:145
  435.9 1.7 fusion.47
  (65 shorter events, 2.1 us)
Async XLA Ops:
  7.2 27.7 %copy-start = (bf16[4096,8]{0,1:T(8,128)(2,1)S(1)}, bf16[4096,8]{0,1:T(8,128)(2,1)}, u32[]{:S(2)}) copy-start(bf16[4096,8]{0,1:T(8,128)(2,1)} %param.16) | copy-start | bytes 196612
  7.2 2.9 copy-start.13
  7.2 27.7 %all-gather.5.cloned.1.call-start = ((), (), s32[]{:S(2)}) async-start(), calls=%async_computation | async-start | bytes 2621440 | tf_op jit(solution)/shard_map/all_gather | solution.py:67
  7.9 109.3 %all-gather.9.cloned.1.call-start = ((), (), s32[]{:S(2)}) async-start(), calls=%async_computation.2 | async-start | bytes 5242880 | tf_op jit(solution)/shard_map/all_gather | solution.py:70
  8.7 28.6 %copy-start.10 = (bf16[4096,8]{0,1:T(8,128)(2,1)S(1)}, bf16[4096,8]{0,1:T(8,128)(2,1)}, u32[]{:S(2)}) copy-start(bf16[4096,8]{0,1:T(8,128)(2,1)} %param.17) | copy-start | bytes 196612
  8.7 189.4 %all-gather.11.cloned.1.call-start = ((), (), s32[]{:S(2)}) async-start(), calls=%async_computation.3 | async-start | bytes 5242880 | tf_op jit(solution)/shard_map/all_gather | solution.py:69
  9.4 269.3 %all-gather.7.cloned.1.call-start = ((), (), s32[]{:S(2)}) async-start(), calls=%async_computation.1 | async-start | bytes 5242880 | tf_op jit(solution)/shard_map/all_gather | solution.py:71
  10.0 425.9 %all-reduce.3.cloned.1.call-start = ((), (), s32[]{:S(2)}) async-start(), calls=%async_computation.4 | async-start | bytes 524288 | tf_op jit(solution)/shard_map/psum | solution.py:145
  34.9 2.4 copy-start.1
  120.9 80.7 %copy-start.11 = (bf16[8,512]{1,0:T(8,128)(2,1)S(1)}, bf16[8,512]{1,0:T(8,128)(2,1)}, u32[]{:S(2)}) copy-start(bf16[8,512]{1,0:T(8,128)(2,1)} %param.18) | copy-start | bytes 24580
  203.8 78.4 %copy-start.12 = (bf16[8,512]{1,0:T(8,128)(2,1)S(1)}, bf16[8,512]{1,0:T(8,128)(2,1)}, u32[]{:S(2)}) copy-start(bf16[8,512]{1,0:T(8,128)(2,1)} %param.19) | copy-start | bytes 24580
  284.2 0.9 copy-start.2
  284.2 1.0 copy-start.5
  287.3 15.5 %collective-permute-start = (bf16[2,256,4,128]{3,1,2,0:T(8,128)(2,1)}, bf16[2,256,4,128]{3,1,2,0:T(8,128)(2,1)S(1)}, u32[]{:S(2)}, u32[]{:S(2)}) collective-permute-start(bf16[2,256,4,128]{3,1,2,0:T(8,128)(2,1)} %pad_maximum_fusion), channel_id=1, source_target_pairs={{12,0},{0,4},{4,8},{8,12},{13,1},{1,5},{5,9},{9,13},{14,2},{2,6},{... | collective-permute-start | bytes 1572872 | tf_op jit(solution)/shard_map/ppermute | solution.py:17
  303.6 4.8 %copy-start.7 = (bf16[256,512]{0,1:T(8,128)(2,1)S(1)}, bf16[256,512]{0,1:T(8,128)(2,1)}, u32[]{:S(2)}) copy-start(bf16[256,512]{0,1:T(8,128)(2,1)} %copy.34) | copy-start | bytes 786436
  308.4 3.1 copy-start.8
  308.4 3.1 copy-start.9
  308.4 3.1 copy-start.14
  315.5 2.2 copy-start.3
  315.5 2.2 copy-start.4
  317.7 13.0 %collective-permute-start.1 = (f32[256,512]{0,1:T(8,128)}, f32[256,512]{0,1:T(8,128)}, u32[]{:S(2)}, u32[]{:S(2)}) collective-permute-start(f32[256,512]{0,1:T(8,128)} %bitcast.14), channel_id=1, source_target_pairs={{4,0},{8,4},{12,8},{0,12},{5,1},{9,5},{13,9},{1,13},{6,2},{10,6},{... | collective-permute-start | bytes 1572872 | tf_op jit(solution)/shard_map/ppermute | solution.py:17
  318.0 14.0 %copy-start.6 = (f32[8,512,16]{1,0,2:T(8,128)S(1)}, f32[8,512,16]{1,0,2:T(8,128)}, u32[]{:S(2)}) copy-start(f32[8,512,16]{1,0,2:T(8,128)} %custom-call) | copy-start | bytes 786436
Sparse Core Ops, SparseCore 0:
  9.6 25.2 all-gather.4
  36.5 80.7 all-gather.8
  118.8 79.2 all-gather.10
  199.5 79.2 all-gather.6
  346.4 89.4 all-reduce.2
where the time goes:
time: 445 us; the launch traced here: 444 us
  waiting for transfers between devices  352 us (79%)
  matrix products  28.9 us (6%)
  local copies, waits for them, and re-layouts  20.4 us (5%)
  blocking collectives  18.4 us (4%)
  between operations  14.1 us (3%)
  loops' own time  5.47 us (1%)
  other arithmetic  5.13 us (1%)
    all_gather x1, waiting for transfers between devices, local(): lax.all_gather(w_key, 'ctx', axis=0, tiled=True)  79.3 us
    all_gather x1, waiting for transfers between devices, local(): lax.all_gather(w_query, 'ctx', axis=0, tiled=True)  77.2 us
    all_gather x1, waiting for transfers between devices, local(): lax.all_gather(w_value, 'ctx', axis=0, tiled=True)  74.9 us
    psum x1, waiting for transfers between devices, local(): lax.psum(project_back(full_states, low_grads), ('ctx', 'head', 'sub'))  71.1 us
    all_gather x1, waiting for transfers between devices, local(): lax.all_gather(hidden_states, ('head', 'sub'), axis=1, tiled=True)  23.4 us
    ppermute x2, waiting for transfers between devices, passed_along(): return lax.ppermute(block, axis, route)  23.1 us
    psum x1, blocking collectives, local(): grad_bq, grad_bv = lax.psum((grad_bq, grad_bv), 'ctx')  18.4 us
    dot_general x3, matrix products, local(): jnp.dot(full_states, weights_piece, preferred_element_type=jnp.float32)  10.3 us
  transfers between devices with their start and end apart: 7, of which 7 were waited for; matrix products, arithmetic and copies ran while one was open for 4% of the time, Pallas kernels for 0%

commit v1 on v0

--- a/solution.py
+++ b/solution.py
@@ -1,8 +1,11 @@
+import functools
 import math
 
 import jax
 import jax.numpy as jnp
 from jax import lax
+from jax.experimental import pallas as pl
+from jax.experimental.pallas import tpu as pltpu
 from jax.sharding import PartitionSpec as P
 
 HEAD_DIM = 128
@@ -153,6 +156,572 @@
     )
 
 
+LANES = 128
+MESH = pl.DeviceIdType.MESH
+
+
+def one_head_kernel(
+    n,
+    subs,
+    wide,
+    hid_ref,
+    wq_ref,
+    wk_ref,
+    wv_ref,
+    a_ref,
+    bq_ref,
+    bv_ref,
+    pos_ref,
+    og_ref,
+    inv_ref,
+    out_ref,
+    gb_ref,
+    ga_ref,
+    hbuf,
+    wbuf,
+    ogbuf,
+    posbuf,
+    ctab,
+    stab,
+    qbuf,
+    kbuf,
+    vbuf,
+    lowbuf,
+    dqbuf,
+    dvbuf,
+    obuf,
+    outbuf,
+    gbsend,
+    gbrecv,
+    rsend,
+    rrecv,
+    total,
+    agbuf,
+    local_sem,
+    hz_send,
+    hx_send,
+    hs_send,
+    h_recv,
+    w_send,
+    wy_send,
+    w_recv,
+    og_send,
+    og_recv,
+    pos_send,
+    pos_recv,
+    out_send,
+    out_recv,
+    gb_send,
+    gb_recv,
+    rs_send,
+    rs_recv,
+    ag_send,
+    ag_recv,
+):
+    f32, bf16 = jnp.float32, jnp.bfloat16
+    rows, width = hid_ref.shape
+    depth = wq_ref.shape[0]
+    half = depth // 2
+    tokens = rows * n
+    group = tokens // 4
+    r, c = lax.axis_index("rep"), lax.axis_index("ctx")
+    h, s = lax.axis_index("head"), lax.axis_index("sub")
+    hs = h * subs + s
+    members = n * wide
+    me = c * wide + hs
+    weights = (wq_ref, wk_ref, wv_ref)
+    pending = []
+
+    def member(number):
+        col = lax.rem(number, wide)
+        return {"ctx": number // wide, "head": col // subs, "sub": lax.rem(col, subs)}
+
+    def remote(src, dst, send, recv, device):
+        return pltpu.make_async_remote_copy(
+            src_ref=src, dst_ref=dst, send_sem=send, recv_sem=recv, device_id=device, device_id_type=MESH
+        )
+
+    def launch(copy, cond=None):
+        if cond is None:
+            copy.start()
+        else:
+            pl.when(cond)(copy.start)
+        pending.append((copy, cond))
+
+    barrier = pltpu.get_barrier_semaphore()
+    for k in range(1, members):
+        pl.semaphore_signal(
+            barrier, inc=1, device_id=member(lax.rem(me + k, members)), device_id_type=MESH
+        )
+    pl.semaphore_signal(barrier, inc=1, device_id={"rep": 1 - r}, device_id_type=MESH)
+
+    def cols(number, size):
+        return pl.ds(pl.multiple_of(number * size, LANES), size)
+
+    def part(number, size):
+        return pl.ds(pl.multiple_of(number * size, 8), size)
+
+    def hblk(block, column):
+        return hbuf.at[part(block, rows), cols(column, width)]
+
+    def wblk(block, which, side):
+        return wbuf.at[
+            pl.ds(pl.multiple_of(block * depth + side * half, 8), half), pl.ds(which * LANES, LANES)
+        ]
+
+    locals_ = [
+        pltpu.make_async_copy(hid_ref, hblk(c, hs), local_sem.at[0]),
+        pltpu.make_async_copy(a_ref, wbuf.at[:, pl.ds(3 * LANES, LANES)], local_sem.at[1]),
+        pltpu.make_async_copy(og_ref.at[:, cols(c, LANES)], ogbuf.at[part(c, rows), :], local_sem.at[2]),
+        pltpu.make_async_copy(pos_ref, posbuf.at[c], local_sem.at[3]),
+    ]
+    for m in range(3):
+        locals_.append(
+            pltpu.make_async_copy(
+                weights[m].at[:, cols(c, LANES)],
+                wbuf.at[part(c, depth), pl.ds(m * LANES, LANES)],
+                local_sem.at[4 + m],
+            )
+        )
+    for copy in locals_:
+        copy.start()
+    pl.semaphore_wait(barrier, members)
+
+    def spread(src, block):
+        launch(
+            remote(src, hblk(block, hs), hx_send.at[block], h_recv.at[block, hs], {"head": 1 - h})
+        )
+        launch(
+            remote(src, hblk(block, hs), hs_send.at[0, block], h_recv.at[block, hs], {"sub": 1 - s})
+        )
+
+    def arrived(block, column):
+        return remote(
+            hblk(block, column), hblk(block, column), hx_send.at[0], h_recv.at[block, column], {"sub": 1 - s}
+        )
+
+    def go_up(src, block):
+        return remote(src, hblk(block, hs), hz_send.at[0, block], h_recv.at[block, hs], {"ctx": c + 1})
+
+    def go_down(src, block):
+        return remote(src, hblk(block, hs), hz_send.at[1, block], h_recv.at[block, hs], {"ctx": c - 1})
+
+    def send_w(t, sign):
+        target = c + sign * t
+        cond = (target < n) if sign > 0 else (target >= 0)
+        slot = 2 * (t - 1) + (1 if sign > 0 else 0)
+        for m in range(3):
+            launch(
+                remote(
+                    weights[m].at[pl.ds(pl.multiple_of(r * half, 8), half), cols(target, LANES)],
+                    wblk(c, m, r),
+                    w_send.at[slot, m],
+                    w_recv.at[c, m, r],
+                    {"ctx": target},
+                ),
+                cond,
+            )
+
+    def pass_w(block, cond):
+        for m in range(3):
+            copy = remote(
+                wblk(block, m, r), wblk(block, m, r), wy_send.at[block, m], w_recv.at[block, m, r], {"rep": 1 - r}
+            )
+
+            @pl.when(cond)
+            def _():
+                copy.wait_recv()
+                copy.start()
+
+            pending.append((copy, cond))
+
+    def pass_x(block, cond):
+        copy = remote(
+            hblk(block, (1 - h) * subs + s),
+            hblk(block, (1 - h) * subs + s),
+            hs_send.at[1, block],
+            h_recv.at[block, (1 - h) * subs + s],
+            {"sub": 1 - s},
+        )
+
+        def act():
+            copy.wait_recv()
+            copy.start()
+
+        if cond is None:
+            act()
+        else:
+            pl.when(cond)(act)
+        pending.append((copy, cond))
+
+    launch(go_up(hid_ref, c), c < n - 1)
+    launch(go_down(hid_ref, c), c > 0)
+    spread(hid_ref, c)
+    for t in range(1, n):
+        for sign in (1, -1):
+            target = c + sign * t
+            cond = (target < n) if sign > 0 else (target >= 0)
+            slot = 2 * (t - 1) + (1 if sign > 0 else 0)
+            launch(
+                remote(pos_ref, posbuf.at[c], pos_send.at[slot], pos_recv.at[c], {"ctx": target}), cond
+            )
+            launch(
+                remote(
+                    og_ref.at[:, cols(target, LANES)],
+                    ogbuf.at[part(c, rows), :],
+                    og_send.at[slot],
+                    og_recv.at[c],
+                    {"ctx": target},
+                ),
+                cond,
+            )
+    send_w(1, 1)
+    send_w(1, -1)
+    pass_x(c, None)
+
+    def hidden_step(t):
+        low_block, high_block = c - t, c + t
+
+        @pl.when(low_block >= 0)
+        def _():
+            arrived(low_block, hs).wait_recv()
+
+        for copy_of, block, cond, more in (
+            (go_up, low_block, low_block >= 0, c < n - 1),
+            (go_down, high_block, high_block < n, c > 0),
+        ):
+            if copy_of is go_down:
+
+                @pl.when(cond)
+                def _():
+                    arrived(high_block, hs).wait_recv()
+
+            launch(copy_of(hblk(block, hs), block), cond & more)
+            for copy in (
+                remote(hblk(block, hs), hblk(block, hs), hx_send.at[block], h_recv.at[block, hs], {"head": 1 - h}),
+                remote(hblk(block, hs), hblk(block, hs), hs_send.at[0, block], h_recv.at[block, hs], {"sub": 1 - s}),
+            ):
+                launch(copy, cond)
+
+    def x_step(t):
+        pass_x(c - t, c - t >= 0)
+        pass_x(c + t, c + t < n)
+
+    def w_step(t):
+        pass_w(c - t, c - t >= 0)
+        pass_w(c + t, c + t < n)
+
+    def tables():
+        for block in range(n):
+
+            @pl.when(block != c)
+            def _():
+                remote(pos_ref, posbuf.at[block], pos_send.at[0], pos_recv.at[block], {"sub": 1 - s}).wait_recv()
+
+        locals_[3].wait()
+        lane = lax.broadcasted_iota(jnp.int32, (LANES, LANES), 1)
+        chunks = rows // LANES
+
+        def one(number, carry):
+            row = posbuf[number // chunks, pl.ds(lax.rem(number, chunks), 1), :].astype(f32)
+            column = jnp.transpose(jnp.broadcast_to(row, (LANES, LANES)))
+            angle = (column * (TRAIN_CTX / MAX_POS)) * inv_ref[0:1, :]
+            here = part(number, LANES)
+            ctab[here, :] = jnp.cos(angle)
+            sine = jnp.sin(angle)
+            stab[here, :] = jnp.where(lane < LANES // 2, -sine, sine)
+            return carry
+
+        lax.fori_loop(0, tokens // LANES, one, 0)
+
+    for t in range(1, n):
+        hidden_step(t)
+        if t + 1 < n:
+            send_w(t + 1, 1)
+            send_w(t + 1, -1)
+        if t == 1:
+            tables()
+        x_step(t)
+        if t > 1:
+            w_step(t - 1)
+    w_step(n - 1)
+
+    for block in range(n):
+        for column in range(wide):
+            mine = (column // subs == h) & (column % subs == s)
+            across = (column // subs != h) & (column % subs == s)
+
+            @pl.when(jnp.logical_not(mine | across))
+            def _():
+                arrived(block, column).wait_recv()
+
+        @pl.when(block != c)
+        def _():
+            for m in range(3):
+                remote(
+                    wblk(block, m, 1 - r), wblk(block, m, 1 - r), wy_send.at[0, 0], w_recv.at[block, m, 1 - r], {"rep": 1 - r}
+                ).wait_recv()
+            remote(
+                ogbuf.at[part(block, rows), :], ogbuf.at[part(block, rows), :], og_send.at[0], og_recv.at[block], {"sub": 1 - s}
+            ).wait_recv()
+
+    for number, copy in enumerate(locals_):
+        if number != 3:
+            copy.wait()
+
+    def turn(u, cosine, sine):
+        return u * cosine + pltpu.roll(u, LANES // 2, 1) * sine
+
+    def project(block, carry):
+        here = part(block, rows)
+        y = jnp.dot(hbuf[here, :], wbuf[...], preferred_element_type=f32)
+        low = y[:, 3 * LANES :].astype(bf16)
+        lowbuf[here, :] = low
+        cosine, sine = ctab[here, :], stab[here, :]
+        pre_q = y[:, :LANES] + 2.0 * jnp.dot(low, bq_ref[...], preferred_element_type=f32)
+        qbuf[here, :] = turn(pre_q, cosine, sine).astype(bf16)
+        kbuf[here, :] = turn(y[:, LANES : 2 * LANES], cosine, sine).astype(bf16)
+        vbuf[here, :] = (
+            y[:, 2 * LANES : 3 * LANES] + 2.0 * jnp.dot(low, bv_ref[...], preferred_element_type=f32)
+        ).astype(bf16)
+        return carry
+
+    lax.fori_loop(0, n, project, 0)
+
+    shift = jnp.where(hs * n + c >= HEADS // 2, group // 2, 0)
+    scale = 1.0 / math.sqrt(HEAD_DIM)
+    hg = group // 2
+    dot_t = functools.partial(
+        lax.dot_general, dimension_numbers=(((1,), (1,)), ((), ())), preferred_element_type=f32
+    )
+    t_dot = functools.partial(
+        lax.dot_general, dimension_numbers=(((0,), (0,)), ((), ())), preferred_element_type=f32
+    )
+    allowed = lax.broadcasted_iota(jnp.int32, (group, group), 0) >= lax.broadcasted_iota(
+        jnp.int32, (group, group), 1
+    )
+
+    def attend(g, carry):
+        first = pl.ds(pl.multiple_of(lax.rem(g * group + shift, tokens), 8), hg)
+        second = pl.ds(pl.multiple_of(lax.rem(g * group + hg + shift, tokens), 8), hg)
+
+        def take(ref):
+            return jnp.concatenate([ref[first, :], ref[second, :]], axis=0)
+
+        def put(ref, value):
+            ref[first, :] = value[:hg]
+            ref[second, :] = value[hg:]
+
+        q, k, v, grad = take(qbuf), take(kbuf), take(vbuf), take(ogbuf)
+        scores = jnp.where(allowed, dot_t(q, k) * scale, -jnp.inf)
+        highest = jnp.max(scores, axis=-1, keepdims=True)
+        expo = jnp.where(allowed, jnp.exp(scores - highest), 0.0)
+        probs = expo / jnp.sum(expo, axis=-1, keepdims=True)
+        probs_b = probs.astype(bf16)
+        out = jnp.dot(probs_b, v, preferred_element_type=f32).astype(bf16)
+        put(obuf, out)
+        dprob = dot_t(grad, v)
+        delta = jnp.sum(grad.astype(f32) * out.astype(f32), axis=-1, keepdims=True)
+        dscore_b = (probs * (dprob - delta) * scale).astype(bf16)
+        dq = jnp.dot(dscore_b, k, preferred_element_type=f32)
+        put(dqbuf, turn(dq, take(ctab), -take(stab)).astype(bf16))
+        put(dvbuf, t_dot(probs_b, grad).astype(bf16))
+        return carry
+
+    lax.fori_loop(0, tokens // group, attend, 0)
+
+    dq, dv, low = dqbuf[...], dvbuf[...], lowbuf[...]
+    low_t = 2.0 * (dot_t(bq_ref[0:16, :], dq) + dot_t(bv_ref[0:16, :], dv))
+    for k in range(members):
+        at = (k // 2) * LANES
+        rsend[k] = low_t[8 * (k % 2) : 8 * (k % 2) + 8, at : at + LANES]
+    for k in range(1, members):
+        to = lax.rem(me + k, members)
+        launch(remote(rsend.at[to], rrecv.at[me], rs_send.at[k], rs_recv.at[me], member(to)))
+    for t in range(1, n):
+        for sign in (1, -1):
+            target = c + sign * t
+            cond = (target < n) if sign > 0 else (target >= 0)
+            slot = 2 * (t - 1) + (1 if sign > 0 else 0)
+            launch(
+                remote(
+                    obuf.at[part(target, rows), :], outbuf.at[c], out_send.at[slot], out_recv.at[c], {"ctx": target}
+                ),
+                cond,
+            )
+    gbsend[0:8, :] = (2.0 * t_dot(low, dq))[0:8]
+    gbsend[8:16, :] = (2.0 * t_dot(low, dv))[8:16]
+    out_ref[:, cols(c, LANES)] = obuf[part(c, rows), :]
+    gb_ref[:, cols(c, LANES)] = gbsend[...]
+
+    rrecv[me] = rsend[me]
+    for k in range(1, members):
+        frm = lax.rem(me + k, members)
+        remote(rsend.at[0], rrecv.at[frm], rs_send.at[0], rs_recv.at[frm], {"sub": 1 - s}).wait_recv()
+    reduced = rrecv[0]
+    for k in range(1, members):
+        reduced = reduced + rrecv[k]
+    total[...] = reduced
+    agbuf[me] = reduced
+    for k in range(1, members):
+        to = lax.rem(me + k, members)
+        launch(remote(total, agbuf.at[me], ag_send.at[k], ag_recv.at[me], member(to)))
+    for t in range(1, n):
+        for sign in (1, -1):
+            target = c + sign * t
+            cond = (target < n) if sign > 0 else (target >= 0)
+            slot = 2 * (t - 1) + (1 if sign > 0 else 0)
+            launch(
+                remote(gbsend, gbrecv.at[c], gb_send.at[slot], gb_recv.at[c], {"ctx": target}), cond
+            )
+    for block in range(n):
+
+        @pl.when(block != c)
+        def _():
+            remote(gbsend, gbrecv.at[block], gb_send.at[0], gb_recv.at[block], {"sub": 1 - s}).wait_recv()
+            remote(outbuf.at[block], outbuf.at[block], out_send.at[0], out_recv.at[block], {"sub": 1 - s}).wait_recv()
+            gb_ref[:, block * LANES : (block + 1) * LANES] = gbrecv[block]
+            out_ref[:, block * LANES : (block + 1) * LANES] = outbuf[block]
+
+    for k in range(1, members):
+        frm = lax.rem(me + k, members)
+        remote(total, agbuf.at[frm], ag_send.at[0], ag_recv.at[frm], {"sub": 1 - s}).wait_recv()
+    full = jnp.concatenate(
+        [
+            jnp.concatenate([agbuf[2 * k + side] for k in range(members // 2)], axis=1)
+            for side in range(2)
+        ],
+        axis=0,
+    )
+    upper = full.astype(bf16)
+    lower = (full - upper.astype(f32)).astype(bf16)
+    both = jnp.concatenate([upper, lower], axis=0)
+    tile = 512
+
+    def back(number, carry):
+        here = pl.ds(pl.multiple_of(number * tile, LANES), tile)
+        product = jnp.dot(both, hbuf[:, here], preferred_element_type=f32)
+        ga_ref[:, here] = product[0:16] + product[16:32]
+        return carry
+
+    lax.fori_loop(0, hbuf.shape[1] // tile, back, 0)
+    for copy, cond in pending:
+        if cond is None:
+            copy.wait_send()
+        else:
+            pl.when(cond)(copy.wait_send)
+
+
+def one_head(
+    hidden_states, w_query, w_key, w_value, a_query, a_value, b_query, b_value, positions, out_grad
+):
+    f32, bf16 = jnp.float32, jnp.bfloat16
+    n, subs = lax.axis_size("ctx"), lax.axis_size("sub")
+    wide = subs * lax.axis_size("head")
+    rows, width = hidden_states.shape
+    model = a_query.shape[0]
+    rank = a_query.shape[1]
+    tokens = rows * n
+    columns = w_query.shape[1]
+    members = n * wide
+    c = lax.axis_index("ctx")
+    a_pad = jnp.pad(jnp.concatenate([a_query, a_value], axis=1), ((0, 0), (0, LANES - 2 * rank)))
+    bq = lax.dynamic_slice_in_dim(b_query, c * LANES, LANES, 1)
+    bv = lax.dynamic_slice_in_dim(b_value, c * LANES, LANES, 1)
+    bq = jnp.pad(bq, ((0, LANES - rank), (0, 0)))
+    bv = jnp.pad(bv, ((rank, LANES - 2 * rank), (0, 0)))
+    half_dim = HEAD_DIM // 2
+    inverse = jnp.exp(
+        jnp.arange(half_dim, dtype=f32) * (-2.0 * math.log(10000.0) / HEAD_DIM)
+    )
+    inverse = jnp.broadcast_to(jnp.concatenate([inverse, inverse])[None, :], (8, LANES))
+    pos = positions.reshape(rows // LANES, LANES)
+    pos = jnp.pad(pos, ((0, 8 - rows // LANES), (0, 0)))
+    vmem, dma = pltpu.VMEM, pltpu.SemaphoreType.DMA
+    hbm_spec = pl.BlockSpec(memory_space=pl.ANY)
+    vmem_spec = pl.BlockSpec(memory_space=pltpu.VMEM)
+    out, gb, ga = pl.pallas_call(
+        functools.partial(one_head_kernel, n, subs, wide),
+        out_shape=(
+            jax.ShapeDtypeStruct((rows, columns), bf16),
+            jax.ShapeDtypeStruct((2 * rank, columns), f32),
+            jax.ShapeDtypeStruct((2 * rank, model), f32),
+        ),
+        in_specs=[hbm_spec] * 5 + [vmem_spec] * 2 + [hbm_spec] * 2 + [vmem_spec],
+        out_specs=[vmem_spec] * 3,
+        scratch_shapes=[
+            vmem((tokens, model), bf16),
+            vmem((model, 4 * LANES), bf16),
+            vmem((tokens, LANES), bf16),
+            vmem((n, 8, LANES), jnp.int32),
+            vmem((tokens, LANES), f32),
+            vmem((tokens, LANES), f32),
+            vmem((tokens, LANES), bf16),
+            vmem((tokens, LANES), bf16),
+            vmem((tokens, LANES), bf16),
+            vmem((tokens, LANES), bf16),
+            vmem((tokens, LANES), bf16),
+            vmem((tokens, LANES), bf16),
+            vmem((tokens, LANES), bf16),
+            vmem((n, rows, LANES), bf16),
+            vmem((2 * rank, LANES), f32),
+            vmem((n, 2 * rank, LANES), f32),
+            vmem((members, 8, LANES), f32),
+            vmem((members, 8, LANES), f32),
+            vmem((8, LANES), f32),
+            vmem((members, 8, LANES), f32),
+            dma((7,)),
+            dma((2, n)),
+            dma((n,)),
+            dma((2, n)),
+            dma((n, wide)),
+            dma((2 * n, 3)),
+            dma((n, 3)),
+            dma((n, 3, 2)),
+            dma((2 * n,)),
+            dma((n,)),
+            dma((2 * n,)),
+            dma((n,)),
+            dma((2 * n,)),
+            dma((n,)),
+            dma((2 * n,)),
+            dma((n,)),
+            dma((members,)),
+            dma((members,)),
+            dma((members,)),
+            dma((members,)),
+        ],
+        compiler_params=pltpu.CompilerParams(
+            collective_id=0, has_side_effects=True, vmem_limit_bytes=56 * 1024 * 1024
+        ),
+    )(hidden_states, w_query, w_key, w_value, a_pad, bq, bv, pos, out_grad, inverse)
+    return (out, ga[:rank].T, gb[:rank], ga[rank:].T, gb[rank:])
+
+
+def fits_one_head(mesh, args):
+    hidden_states, w_query, a_query = args[0], args[1], args[4]
+    n = mesh.shape["ctx"]
+    heads_here = w_query.shape[1] // HEAD_DIM
+    rows = hidden_states.shape[0]
+    members = n * mesh.shape["head"] * mesh.shape["sub"]
+    return (
+        mesh.shape["rep"] == 2
+        and mesh.shape["head"] == 2
+        and mesh.shape["sub"] == 2
+        and heads_here == n
+        and HEAD_DIM == LANES
+        and a_query.shape[1] == 8
+        and rows % LANES == 0
+        and rows // LANES <= 8
+        and 2 * rows * n // LANES == members
+        and rows * n * a_query.shape[0] <= 2**22
+    )
+
+
+def choose(mesh, *args):
+    return one_head(*args) if fits_one_head(mesh, args) else local(*args)
+
+
 def solution(mesh):
     in_specs = (
         P(("rep", "ctx"), ("head", "sub")),
@@ -173,4 +742,6 @@
         P(None, "rep"),
         P("rep", ("head", "sub")),
     )
-    return jax.shard_map(local, mesh=mesh, in_specs=in_specs, out_specs=out_specs, check_vma=False)
+    return jax.shard_map(
+        functools.partial(choose, mesh), mesh=mesh, in_specs=in_specs, out_specs=out_specs, check_vma=False
+    )

time: 445 us -> 148 us (0.33)
  waiting for transfers between devices: 352 us -> 0 us
  Pallas kernels: 0 us -> 138 us
  matrix products: 28.9 us -> 0 us
  blocking collectives: 18.4 us -> 0 us
  between operations: 14.1 us -> 0.67 us
  local copies, waits for them, and re-layouts: 20.4 us -> 8.53 us
  loops' own time: 5.47 us -> 0 us
    all_gather x4 -> x0, waiting for transfers between devices: 255 us -> none  [the longest x1 79.3 us: local(): lax.all_gather(w_key, 'ctx', axis=0, tiled=True)]
    pallas_call x0 -> x1, Pallas kernels: none -> 138 us  [one_head(): pl.pallas_call(functools.partial(one_head_kernel, n, subs, wide), out_sha...]
    psum x1 -> x0, waiting for transfers between devices: 71.1 us -> none  [local(): lax.psum(project_back(full_states, low_grads), ('ctx', 'head', 'sub'))]
    dot_general x22 -> x0, matrix products: 24.2 us -> none  [the longest x3 10.3 us: local(): jnp.dot(full_states, weights_piece, preferred_element_type=jnp.float32)]
    ppermute x2 -> x0, waiting for transfers between devices: 23.1 us -> none  [passed_along(): return lax.ppermute(block, axis, route)]
    psum x1 -> x0, blocking collectives: 18.4 us -> none  [local(): grad_bq, grad_bv = lax.psum((grad_bq, grad_bv), 'ctx')]
    another operation x1 -> x0, loops' own time: 5.47 us -> none  [project_back(): blocks = lax.map(one_block, jnp.arange(block_count))]
    sub x1 -> x0, matrix products: 4.75 us -> none  [local(): expo = jnp.where(visible, jnp.exp(scores - highest), 0.0)]
  transfers between devices with their start and end apart: 7 -> 0, of which waited for: 7 -> 0; matrix products, arithmetic and copies ran while one was open for 4% -> 0% of each run, Pallas kernels for 0% -> 0%
where the time goes in v1:
time: 148 us
  Pallas kernels  138 us (93%)
  local copies, waits for them, and re-layouts  8.53 us (6%)
    pallas_call x1, Pallas kernels, one_head(): pl.pallas_call(functools.partial(one_head_kernel, n, subs, wide), out_sha...  138 us

profile of v1, /device:TPU:0, one launch (start us, length us, event | category | flops | bytes accessed | tf_op | source)
XLA Modules:
  0.0 147.7 jit_solution(13804103599197026959)
XLA Ops:
  0.6 0.9 pad_maximum_fusion
  1.5 0.5 copy.17
  2.0 1.2 pad.16.a_ref
  3.2 0.7 constant_dynamic-slice_fusion
  3.9 0.6 pad.17.bq_ref
  4.5 0.6 pad.18.bv_ref
  5.1 0.0 copy-start.2
  5.1 0.7 copy-done.2
  5.8 0.6 pad.19.pos_ref
  6.4 0.1 pad_maximum_fusion.1
  6.5 0.6 broadcast_in_dim.2.inv_ref
  7.1 137.5 %shard_map.137 = (bf16[256,512]{1,0:T(8,128)(2,1)}, f32[16,512]{1,0:T(8,128)}, f32[16,4096]{1,0:T(8,128)}) custom-call(bf16[256,1024]{1,0:T(8,128)(2,1)} %hid_ref.1, bf16[1024,512]{1,0:T(8,128)(2,1)} %wq_ref.1, bf16[1024,512]{1,0:T(8,128)(2,1)} %wk_ref.1, bf16[1024,512]{1,0:T(8,128)(2,1)} %wv_ref.1, bf16[4096,128]{1,0:T(8,128)(2,1)} %pad.16.a_ref, ...), custom_call_target="tpu_custom_call" | custom-call | tf_op jit(solution)/shard_map/pallas_call | solution.py:643
  144.6 0.0 copy-start.1
  144.6 0.0 copy-start
  144.6 1.7 %slice_bitcast_fusion = (f32[4096,8]{0,1:T(8,128)}, f32[4096,8]{0,1:T(8,128)}) fusion(f32[16,4096]{1,0:T(8,128)} %get-tuple-element.9), kind=kLoop, calls=%fused_computation.1 | loop fusion | bytes 524288 | tf_op jit(solution)/shard_map/transpose | solution.py:698
  146.4 0.0 copy-done.1
  146.4 0.6 fusion
  147.0 0.0 copy-done
  147.0 0.7 copy.19
  (1 shorter events, 0.0 us)
Async XLA Ops:
  5.1 0.7 copy-start.2
  144.6 1.8 %copy-start.1 = (f32[16,512]{1,0:T(8,128)S(1)}, f32[16,512]{1,0:T(8,128)}, u32[]{:S(2)}) copy-start(f32[16,512]{1,0:T(8,128)} %get-tuple-element.10) | copy-start | bytes 98308
  144.6 2.4 %copy-start = (bf16[256,512]{1,0:T(8,128)(2,1)S(1)}, bf16[256,512]{1,0:T(8,128)(2,1)}, u32[]{:S(2)}) copy-start(bf16[256,512]{1,0:T(8,128)(2,1)} %get-tuple-element.22) | copy-start | bytes 786436

commit v2 on v1

--- a/solution.py
+++ b/solution.py
@@ -168,15 +168,17 @@
     wq_ref,
     wk_ref,
     wv_ref,
-    a_ref,
+    aq_ref,
+    av_ref,
     bq_ref,
     bv_ref,
     pos_ref,
     og_ref,
-    inv_ref,
     out_ref,
-    gb_ref,
-    ga_ref,
+    gaq_ref,
+    gbq_ref,
+    gav_ref,
+    gbv_ref,
     hbuf,
     wbuf,
     ogbuf,
@@ -186,6 +188,7 @@
     qbuf,
     kbuf,
     vbuf,
+    acc,
     lowbuf,
     dqbuf,
     dvbuf,
@@ -231,6 +234,12 @@
     me = c * wide + hs
     weights = (wq_ref, wk_ref, wv_ref)
     pending = []
+    dot_t = functools.partial(
+        lax.dot_general, dimension_numbers=(((1,), (1,)), ((), ())), preferred_element_type=f32
+    )
+    t_dot = functools.partial(
+        lax.dot_general, dimension_numbers=(((0,), (0,)), ((), ())), preferred_element_type=f32
+    )
 
     def member(number):
         col = lax.rem(number, wide)
@@ -271,16 +280,15 @@
 
     locals_ = [
         pltpu.make_async_copy(hid_ref, hblk(c, hs), local_sem.at[0]),
-        pltpu.make_async_copy(a_ref, wbuf.at[:, pl.ds(3 * LANES, LANES)], local_sem.at[1]),
-        pltpu.make_async_copy(og_ref.at[:, cols(c, LANES)], ogbuf.at[part(c, rows), :], local_sem.at[2]),
-        pltpu.make_async_copy(pos_ref, posbuf.at[c], local_sem.at[3]),
+        pltpu.make_async_copy(og_ref.at[:, cols(c, LANES)], ogbuf.at[part(c, rows), :], local_sem.at[1]),
+        pltpu.make_async_copy(pos_ref, posbuf.at[c], local_sem.at[2]),
     ]
     for m in range(3):
         locals_.append(
             pltpu.make_async_copy(
                 weights[m].at[:, cols(c, LANES)],
                 wbuf.at[part(c, depth), pl.ds(m * LANES, LANES)],
-                local_sem.at[4 + m],
+                local_sem.at[3 + m],
             )
         )
     for copy in locals_:
@@ -357,27 +365,15 @@
     launch(go_up(hid_ref, c), c < n - 1)
     launch(go_down(hid_ref, c), c > 0)
     spread(hid_ref, c)
-    for t in range(1, n):
-        for sign in (1, -1):
-            target = c + sign * t
-            cond = (target < n) if sign > 0 else (target >= 0)
-            slot = 2 * (t - 1) + (1 if sign > 0 else 0)
-            launch(
-                remote(pos_ref, posbuf.at[c], pos_send.at[slot], pos_recv.at[c], {"ctx": target}), cond
-            )
-            launch(
-                remote(
-                    og_ref.at[:, cols(target, LANES)],
-                    ogbuf.at[part(c, rows), :],
-                    og_send.at[slot],
-                    og_recv.at[c],
-                    {"ctx": target},
-                ),
-                cond,
-            )
-    send_w(1, 1)
-    send_w(1, -1)
-    pass_x(c, None)
+    def routes():
+        for t in range(1, n):
+            for sign in (1, -1):
+                target = c + sign * t
+                cond = (target < n) if sign > 0 else (target >= 0)
+                yield 2 * (t - 1) + (1 if sign > 0 else 0), target, cond
+
+    for slot, target, cond in routes():
+        launch(remote(pos_ref, posbuf.at[c], pos_send.at[slot], pos_recv.at[c], {"ctx": target}), cond)
 
     def hidden_step(t):
         low_block, high_block = c - t, c + t
@@ -418,14 +414,17 @@
             def _():
                 remote(pos_ref, posbuf.at[block], pos_send.at[0], pos_recv.at[block], {"sub": 1 - s}).wait_recv()
 
-        locals_[3].wait()
+        locals_[2].wait()
         lane = lax.broadcasted_iota(jnp.int32, (LANES, LANES), 1)
         chunks = rows // LANES
+        half_dim = LANES // 2
+        index = lax.broadcasted_iota(jnp.int32, (8, LANES), 1) % half_dim
+        inverse = jnp.exp(index.astype(f32) * (-2.0 * math.log(10000.0) / HEAD_DIM))[0:1, :]
 
         def one(number, carry):
             row = posbuf[number // chunks, pl.ds(lax.rem(number, chunks), 1), :].astype(f32)
             column = jnp.transpose(jnp.broadcast_to(row, (LANES, LANES)))
-            angle = (column * (TRAIN_CTX / MAX_POS)) * inv_ref[0:1, :]
+            angle = (column * (TRAIN_CTX / MAX_POS)) * inverse
             here = part(number, LANES)
             ctab[here, :] = jnp.cos(angle)
             sine = jnp.sin(angle)
@@ -434,18 +433,32 @@
 
         lax.fori_loop(0, tokens // LANES, one, 0)
 
-    for t in range(1, n):
+    hidden_step(1)
+    send_w(1, 1)
+    send_w(1, -1)
+    pass_x(c, None)
+    for t in range(2, n):
         hidden_step(t)
-        if t + 1 < n:
-            send_w(t + 1, 1)
-            send_w(t + 1, -1)
-        if t == 1:
+        if t == 2:
+            for far in range(2, n):
+                send_w(far, 1)
+                send_w(far, -1)
+            for slot, target, cond in routes():
+                launch(
+                    remote(
+                        og_ref.at[:, cols(target, LANES)],
+                        ogbuf.at[part(c, rows), :],
+                        og_send.at[slot],
+                        og_recv.at[c],
+                        {"ctx": target},
+                    ),
+                    cond,
+                )
+        x_step(t - 1)
+        w_step(t - 1)
+        if t == 2:
             tables()
-        x_step(t)
-        if t > 1:
-            w_step(t - 1)
-    w_step(n - 1)
-
+    x_step(n - 1)
     for block in range(n):
         for column in range(wide):
             mine = (column // subs == h) & (column % subs == s)
@@ -455,34 +468,73 @@
             def _():
                 arrived(block, column).wait_recv()
 
+    for number, copy in enumerate(locals_):
+        if number != 2:
+            copy.wait()
+
+    def gather_low(block, carry):
+        here = part(block, rows)
+        a_both = jnp.concatenate([aq_ref[...].astype(f32), av_ref[...].astype(f32)], axis=0).astype(bf16)
+        lowbuf[here, :] = dot_t(hbuf[here, :], a_both).astype(bf16)
+        return carry
+
+    def multiply(slice_, fresh):
+        deep = cols(slice_, depth)
+
+        def rows_of(block, carry):
+            here = part(block, rows)
+            y = jnp.dot(hbuf[here, deep], wbuf[part(slice_, depth), :], preferred_element_type=f32)
+            if fresh:
+                acc[here, :] = y
+            else:
+                acc[here, :] += y
+            return carry
+
+        lax.fori_loop(0, n, rows_of, 0)
+
+    lax.fori_loop(0, n, gather_low, 0)
+    multiply(c, True)
+    w_step(n - 1)
+    for t in range(1, n):
+        for block, cond in ((c - t, c - t >= 0), (c + t, c + t < n)):
+
+            @pl.when(cond)
+            def _():
+                for m in range(3):
+                    remote(
+                        wblk(block, m, 1 - r),
+                        wblk(block, m, 1 - r),
+                        wy_send.at[0, 0],
+                        w_recv.at[block, m, 1 - r],
+                        {"rep": 1 - r},
+                    ).wait_recv()
+                multiply(block, False)
+
+    for block in range(n):
+
         @pl.when(block != c)
         def _():
-            for m in range(3):
-                remote(
-                    wblk(block, m, 1 - r), wblk(block, m, 1 - r), wy_send.at[0, 0], w_recv.at[block, m, 1 - r], {"rep": 1 - r}
-                ).wait_recv()
             remote(
                 ogbuf.at[part(block, rows), :], ogbuf.at[part(block, rows), :], og_send.at[0], og_recv.at[block], {"sub": 1 - s}
             ).wait_recv()
 
-    for number, copy in enumerate(locals_):
-        if number != 3:
-            copy.wait()
-
     def turn(u, cosine, sine):
         return u * cosine + pltpu.roll(u, LANES // 2, 1) * sine
 
+    empty = jnp.zeros((8, LANES), f32)
+    bq = jnp.concatenate([bq_ref[:, cols(c, LANES)].astype(f32), empty], axis=0).astype(bf16)
+    bv = jnp.concatenate([empty, bv_ref[:, cols(c, LANES)].astype(f32)], axis=0).astype(bf16)
+
     def project(block, carry):
         here = part(block, rows)
-        y = jnp.dot(hbuf[here, :], wbuf[...], preferred_element_type=f32)
-        low = y[:, 3 * LANES :].astype(bf16)
-        lowbuf[here, :] = low
+        y = acc[here, :]
+        low = lowbuf[here, :]
         cosine, sine = ctab[here, :], stab[here, :]
-        pre_q = y[:, :LANES] + 2.0 * jnp.dot(low, bq_ref[...], preferred_element_type=f32)
+        pre_q = y[:, :LANES] + 2.0 * jnp.dot(low, bq, preferred_element_type=f32)
         qbuf[here, :] = turn(pre_q, cosine, sine).astype(bf16)
         kbuf[here, :] = turn(y[:, LANES : 2 * LANES], cosine, sine).astype(bf16)
         vbuf[here, :] = (
-            y[:, 2 * LANES : 3 * LANES] + 2.0 * jnp.dot(low, bv_ref[...], preferred_element_type=f32)
+            y[:, 2 * LANES : 3 * LANES] + 2.0 * jnp.dot(low, bv, preferred_element_type=f32)
         ).astype(bf16)
         return carry
 
@@ -491,12 +543,6 @@
     shift = jnp.where(hs * n + c >= HEADS // 2, group // 2, 0)
     scale = 1.0 / math.sqrt(HEAD_DIM)
     hg = group // 2
-    dot_t = functools.partial(
-        lax.dot_general, dimension_numbers=(((1,), (1,)), ((), ())), preferred_element_type=f32
-    )
-    t_dot = functools.partial(
-        lax.dot_general, dimension_numbers=(((0,), (0,)), ((), ())), preferred_element_type=f32
-    )
     allowed = lax.broadcasted_iota(jnp.int32, (group, group), 0) >= lax.broadcasted_iota(
         jnp.int32, (group, group), 1
     )
@@ -531,28 +577,27 @@
     lax.fori_loop(0, tokens // group, attend, 0)
 
     dq, dv, low = dqbuf[...], dvbuf[...], lowbuf[...]
-    low_t = 2.0 * (dot_t(bq_ref[0:16, :], dq) + dot_t(bv_ref[0:16, :], dv))
+    low_t = 2.0 * (dot_t(bq, dq) + dot_t(bv, dv))
     for k in range(members):
         at = (k // 2) * LANES
         rsend[k] = low_t[8 * (k % 2) : 8 * (k % 2) + 8, at : at + LANES]
     for k in range(1, members):
         to = lax.rem(me + k, members)
         launch(remote(rsend.at[to], rrecv.at[me], rs_send.at[k], rs_recv.at[me], member(to)))
-    for t in range(1, n):
-        for sign in (1, -1):
-            target = c + sign * t
-            cond = (target < n) if sign > 0 else (target >= 0)
-            slot = 2 * (t - 1) + (1 if sign > 0 else 0)
-            launch(
-                remote(
-                    obuf.at[part(target, rows), :], outbuf.at[c], out_send.at[slot], out_recv.at[c], {"ctx": target}
-                ),
-                cond,
-            )
     gbsend[0:8, :] = (2.0 * t_dot(low, dq))[0:8]
     gbsend[8:16, :] = (2.0 * t_dot(low, dv))[8:16]
+    for slot, target, cond in routes():
+        launch(
+            remote(
+                obuf.at[part(target, rows), :], outbuf.at[c], out_send.at[slot], out_recv.at[c], {"ctx": target}
+            ),
+            cond,
+        )
+    for slot, target, cond in routes():
+        launch(remote(gbsend, gbrecv.at[c], gb_send.at[slot], gb_recv.at[c], {"ctx": target}), cond)
     out_ref[:, cols(c, LANES)] = obuf[part(c, rows), :]
-    gb_ref[:, cols(c, LANES)] = gbsend[...]
+    gbq_ref[:, cols(c, LANES)] = gbsend[0:8, :]
+    gbv_ref[:, cols(c, LANES)] = gbsend[8:16, :]
 
     rrecv[me] = rsend[me]
     for k in range(1, members):
@@ -566,23 +611,6 @@
     for k in range(1, members):
         to = lax.rem(me + k, members)
         launch(remote(total, agbuf.at[me], ag_send.at[k], ag_recv.at[me], member(to)))
-    for t in range(1, n):
-        for sign in (1, -1):
-            target = c + sign * t
-            cond = (target < n) if sign > 0 else (target >= 0)
-            slot = 2 * (t - 1) + (1 if sign > 0 else 0)
-            launch(
-                remote(gbsend, gbrecv.at[c], gb_send.at[slot], gb_recv.at[c], {"ctx": target}), cond
-            )
-    for block in range(n):
-
-        @pl.when(block != c)
-        def _():
-            remote(gbsend, gbrecv.at[block], gb_send.at[0], gb_recv.at[block], {"sub": 1 - s}).wait_recv()
-            remote(outbuf.at[block], outbuf.at[block], out_send.at[0], out_recv.at[block], {"sub": 1 - s}).wait_recv()
-            gb_ref[:, block * LANES : (block + 1) * LANES] = gbrecv[block]
-            out_ref[:, block * LANES : (block + 1) * LANES] = outbuf[block]
-
     for k in range(1, members):
         frm = lax.rem(me + k, members)
         remote(total, agbuf.at[frm], ag_send.at[0], ag_recv.at[frm], {"sub": 1 - s}).wait_recv()
@@ -601,10 +629,21 @@
     def back(number, carry):
         here = pl.ds(pl.multiple_of(number * tile, LANES), tile)
         product = jnp.dot(both, hbuf[:, here], preferred_element_type=f32)
-        ga_ref[:, here] = product[0:16] + product[16:32]
+        gaq_ref[:, here] = product[0:8] + product[16:24]
+        gav_ref[:, here] = product[8:16] + product[24:32]
         return carry
 
     lax.fori_loop(0, hbuf.shape[1] // tile, back, 0)
+    for block in range(n):
+
+        @pl.when(block != c)
+        def _():
+            remote(gbsend, gbrecv.at[block], gb_send.at[0], gb_recv.at[block], {"sub": 1 - s}).wait_recv()
+            remote(outbuf.at[block], outbuf.at[block], out_send.at[0], out_recv.at[block], {"sub": 1 - s}).wait_recv()
+            gbq_ref[:, block * LANES : (block + 1) * LANES] = gbrecv[block, 0:8, :]
+            gbv_ref[:, block * LANES : (block + 1) * LANES] = gbrecv[block, 8:16, :]
+            out_ref[:, block * LANES : (block + 1) * LANES] = outbuf[block]
+
     for copy, cond in pending:
         if cond is None:
             copy.wait_send()
@@ -624,42 +663,33 @@
     tokens = rows * n
     columns = w_query.shape[1]
     members = n * wide
-    c = lax.axis_index("ctx")
-    a_pad = jnp.pad(jnp.concatenate([a_query, a_value], axis=1), ((0, 0), (0, LANES - 2 * rank)))
-    bq = lax.dynamic_slice_in_dim(b_query, c * LANES, LANES, 1)
-    bv = lax.dynamic_slice_in_dim(b_value, c * LANES, LANES, 1)
-    bq = jnp.pad(bq, ((0, LANES - rank), (0, 0)))
-    bv = jnp.pad(bv, ((rank, LANES - 2 * rank), (0, 0)))
-    half_dim = HEAD_DIM // 2
-    inverse = jnp.exp(
-        jnp.arange(half_dim, dtype=f32) * (-2.0 * math.log(10000.0) / HEAD_DIM)
-    )
-    inverse = jnp.broadcast_to(jnp.concatenate([inverse, inverse])[None, :], (8, LANES))
     pos = positions.reshape(rows // LANES, LANES)
-    pos = jnp.pad(pos, ((0, 8 - rows // LANES), (0, 0)))
     vmem, dma = pltpu.VMEM, pltpu.SemaphoreType.DMA
     hbm_spec = pl.BlockSpec(memory_space=pl.ANY)
     vmem_spec = pl.BlockSpec(memory_space=pltpu.VMEM)
-    out, gb, ga = pl.pallas_call(
+    out, gaq, gbq, gav, gbv = pl.pallas_call(
         functools.partial(one_head_kernel, n, subs, wide),
         out_shape=(
             jax.ShapeDtypeStruct((rows, columns), bf16),
-            jax.ShapeDtypeStruct((2 * rank, columns), f32),
-            jax.ShapeDtypeStruct((2 * rank, model), f32),
+            jax.ShapeDtypeStruct((rank, model), f32),
+            jax.ShapeDtypeStruct((rank, columns), f32),
+            jax.ShapeDtypeStruct((rank, model), f32),
+            jax.ShapeDtypeStruct((rank, columns), f32),
         ),
-        in_specs=[hbm_spec] * 5 + [vmem_spec] * 2 + [hbm_spec] * 2 + [vmem_spec],
-        out_specs=[vmem_spec] * 3,
+        in_specs=[hbm_spec] * 4 + [vmem_spec] * 4 + [hbm_spec] * 2,
+        out_specs=[vmem_spec] * 5,
         scratch_shapes=[
             vmem((tokens, model), bf16),
-            vmem((model, 4 * LANES), bf16),
+            vmem((model, 3 * LANES), bf16),
             vmem((tokens, LANES), bf16),
-            vmem((n, 8, LANES), jnp.int32),
+            vmem((n, rows // LANES, LANES), jnp.int32),
             vmem((tokens, LANES), f32),
             vmem((tokens, LANES), f32),
             vmem((tokens, LANES), bf16),
             vmem((tokens, LANES), bf16),
             vmem((tokens, LANES), bf16),
-            vmem((tokens, LANES), bf16),
+            vmem((tokens, 3 * LANES), f32),
+            vmem((tokens, 2 * rank), bf16),
             vmem((tokens, LANES), bf16),
             vmem((tokens, LANES), bf16),
             vmem((tokens, LANES), bf16),
@@ -670,7 +700,7 @@
             vmem((members, 8, LANES), f32),
             vmem((8, LANES), f32),
             vmem((members, 8, LANES), f32),
-            dma((7,)),
+            dma((6,)),
             dma((2, n)),
             dma((n,)),
             dma((2, n)),
@@ -694,8 +724,10 @@
         compiler_params=pltpu.CompilerParams(
             collective_id=0, has_side_effects=True, vmem_limit_bytes=56 * 1024 * 1024
         ),
-    )(hidden_states, w_query, w_key, w_value, a_pad, bq, bv, pos, out_grad, inverse)
-    return (out, ga[:rank].T, gb[:rank], ga[rank:].T, gb[rank:])
+    )(
+        hidden_states, w_query, w_key, w_value, a_query.T, a_value.T, b_query, b_value, pos, out_grad
+    )
+    return (out, gaq.T, gbq, gav.T, gbv)
 
 
 def fits_one_head(mesh, args):

time: 148 us -> 122 us (0.82)
  Pallas kernels: 138 us -> 117 us
  local copies, waits for them, and re-layouts: 8.53 us -> 4.35 us
    pallas_call x1, Pallas kernels: 138 us -> 117 us  [one_head(): pl.pallas_call(functools.partial(one_head_kernel, n, subs, wide), out_sha...]
    pad x4 -> x0, local copies, waits for them, and re-layouts: 3.02 us -> none  [the longest x1 1.18 us: one_head(): jnp.pad(jnp.concatenate([a_query, a_value], axis=1), ((0, 0), (0, LANES -...]
    unnamed x7 -> x13, local copies, waits for them, and re-layouts: 1.39 us -> 4.35 us
    transpose x1 -> x0, local copies, waits for them, and re-layouts: 1.73 us -> none  [one_head(): return (out, ga[:rank].T, gb[:rank], ga[rank:].T, gb[rank:])]
where the time goes in v2:
time: 122 us
  Pallas kernels  117 us (96%)
  local copies, waits for them, and re-layouts  4.35 us (4%)
    pallas_call x1, Pallas kernels, one_head(): pl.pallas_call(functools.partial(one_head_kernel, n, subs, wide), out_sha...  117 us
    unnamed x13, local copies, waits for them, and re-layouts  4.35 us

profile of v2, /device:TPU:0, one launch (start us, length us, event | category | flops | bytes accessed | tf_op | source)
XLA Modules:
  0.0 122.0 jit_solution(11000248346617688137)
XLA Ops:
  0.6 117.0 %shard_map.137 = (bf16[256,512]{1,0:T(8,128)(2,1)}, f32[8,4096]{1,0:T(8,128)}, f32[8,512]{1,0:T(8,128)}, f32[8,4096]{1,0:T(8,128)}, f32[8,512]{1,0:T(8,128)}) custom-call(bf16[256,1024]{1,0:T(8,128)(2,1)} %hid_ref.1, bf16[1024,512]{1,0:T(8,128)(2,1)} %wq_ref.1, bf16[1024,512]{1,0:T(8,128)(2,1)} %wk_ref.1, bf16[1024,512]{1,0:T(8,128)(2,1)} %wv_ref.1, ...), custom_call_target="tpu_custom_call" | custom-call | tf_op jit(solution)/shard_map/pallas_call | solution.py:670
  117.6 0.0 copy-start.1
  117.6 1.7 %copy.20 = bf16[256,512]{1,0:T(8,128)(2,1)} copy(bf16[256,512]{1,0:T(8,128)(2,1)} %get-tuple-element.20) | data formatting | bytes 524288
  119.3 0.0 copy-done.1
  119.3 0.0 copy-start.3
  119.3 0.0 copy-start
  119.3 0.7 copy.21
  120.0 0.1 copy-done.3
  120.0 0.6 copy.22
  120.7 0.0 copy-done
  120.7 0.0 copy-start.2
  120.7 0.7 copy.23
  121.3 0.1 copy-done.2
  121.4 0.6 copy.24
Async XLA Ops:
  117.6 1.7 %copy-start.1 = (f32[8,4096]{1,0:T(8,128)S(1)}, f32[8,4096]{1,0:T(8,128)}, u32[]{:S(2)}) copy-start(f32[8,4096]{1,0:T(8,128)} %get-tuple-element.11) | copy-start | bytes 393220
  119.3 0.7 copy-start.3
  119.3 1.3 %copy-start = (f32[8,4096]{1,0:T(8,128)S(1)}, f32[8,4096]{1,0:T(8,128)}, u32[]{:S(2)}) copy-start(f32[8,4096]{1,0:T(8,128)} %get-tuple-element.13) | copy-start | bytes 393220
  120.7 0.7 copy-start.2

commit v3 on v2

--- a/solution.py
+++ b/solution.py
@@ -157,6 +157,7 @@
 
 
 LANES = 128
+PIECES = 2
 MESH = pl.DeviceIdType.MESH
 
 
@@ -270,8 +271,11 @@
     def part(number, size):
         return pl.ds(pl.multiple_of(number * size, 8), size)
 
-    def hblk(block, column):
-        return hbuf.at[part(block, rows), cols(column, width)]
+    def hblk(block, column, piece):
+        return hbuf.at[part(block * PIECES + piece, rows // PIECES), cols(column, width)]
+
+    def own_piece(piece):
+        return hid_ref.at[pl.ds(piece * (rows // PIECES), rows // PIECES), :]
 
     def wblk(block, which, side):
         return wbuf.at[
@@ -279,7 +283,7 @@
         ]
 
     locals_ = [
-        pltpu.make_async_copy(hid_ref, hblk(c, hs), local_sem.at[0]),
+        pltpu.make_async_copy(hid_ref, hbuf.at[part(c, rows), cols(hs, width)], local_sem.at[0]),
         pltpu.make_async_copy(og_ref.at[:, cols(c, LANES)], ogbuf.at[part(c, rows), :], local_sem.at[1]),
         pltpu.make_async_copy(pos_ref, posbuf.at[c], local_sem.at[2]),
     ]
@@ -295,24 +299,24 @@
         copy.start()
     pl.semaphore_wait(barrier, members)
 
-    def spread(src, block):
-        launch(
-            remote(src, hblk(block, hs), hx_send.at[block], h_recv.at[block, hs], {"head": 1 - h})
-        )
-        launch(
-            remote(src, hblk(block, hs), hs_send.at[0, block], h_recv.at[block, hs], {"sub": 1 - s})
-        )
-
-    def arrived(block, column):
+    def spread(src, block, piece, cond=None):
+        land, got = hblk(block, hs, piece), h_recv.at[block, hs, piece]
+        launch(remote(src, land, hx_send.at[block, piece], got, {"head": 1 - h}), cond)
+        launch(remote(src, land, hs_send.at[0, block, piece], got, {"sub": 1 - s}), cond)
+
+    def arrived(block, column, piece):
+        land = hblk(block, column, piece)
+        return remote(land, land, hx_send.at[0, 0], h_recv.at[block, column, piece], {"sub": 1 - s})
+
+    def go_up(src, block, piece):
         return remote(
-            hblk(block, column), hblk(block, column), hx_send.at[0], h_recv.at[block, column], {"sub": 1 - s}
-        )
-
-    def go_up(src, block):
-        return remote(src, hblk(block, hs), hz_send.at[0, block], h_recv.at[block, hs], {"ctx": c + 1})
-
-    def go_down(src, block):
-        return remote(src, hblk(block, hs), hz_send.at[1, block], h_recv.at[block, hs], {"ctx": c - 1})
+            src, hblk(block, hs, piece), hz_send.at[0, block, piece], h_recv.at[block, hs, piece], {"ctx": c + 1}
+        )
+
+    def go_down(src, block, piece):
+        return remote(
+            src, hblk(block, hs, piece), hz_send.at[1, block, piece], h_recv.at[block, hs, piece], {"ctx": c - 1}
+        )
 
     def send_w(t, sign):
         target = c + sign * t
@@ -343,13 +347,11 @@
 
             pending.append((copy, cond))
 
-    def pass_x(block, cond):
+    def pass_x(block, cond, piece):
+        column = (1 - h) * subs + s
+        land = hblk(block, column, piece)
         copy = remote(
-            hblk(block, (1 - h) * subs + s),
-            hblk(block, (1 - h) * subs + s),
-            hs_send.at[1, block],
-            h_recv.at[block, (1 - h) * subs + s],
-            {"sub": 1 - s},
+            land, land, hs_send.at[1, block, piece], h_recv.at[block, column, piece], {"sub": 1 - s}
         )
 
         def act():
@@ -362,9 +364,11 @@
             pl.when(cond)(act)
         pending.append((copy, cond))
 
-    launch(go_up(hid_ref, c), c < n - 1)
-    launch(go_down(hid_ref, c), c > 0)
-    spread(hid_ref, c)
+    for piece in range(PIECES):
+        launch(go_up(own_piece(piece), c, piece), c < n - 1)
+        launch(go_down(own_piece(piece), c, piece), c > 0)
+        spread(own_piece(piece), c, piece)
+
     def routes():
         for t in range(1, n):
             for sign in (1, -1):
@@ -376,32 +380,19 @@
         launch(remote(pos_ref, posbuf.at[c], pos_send.at[slot], pos_recv.at[c], {"ctx": target}), cond)
 
     def hidden_step(t):
-        low_block, high_block = c - t, c + t
-
-        @pl.when(low_block >= 0)
-        def _():
-            arrived(low_block, hs).wait_recv()
-
-        for copy_of, block, cond, more in (
-            (go_up, low_block, low_block >= 0, c < n - 1),
-            (go_down, high_block, high_block < n, c > 0),
-        ):
-            if copy_of is go_down:
-
-                @pl.when(cond)
-                def _():
-                    arrived(high_block, hs).wait_recv()
-
-            launch(copy_of(hblk(block, hs), block), cond & more)
-            for copy in (
-                remote(hblk(block, hs), hblk(block, hs), hx_send.at[block], h_recv.at[block, hs], {"head": 1 - h}),
-                remote(hblk(block, hs), hblk(block, hs), hs_send.at[0, block], h_recv.at[block, hs], {"sub": 1 - s}),
+        for piece in range(PIECES):
+            for go, block, cond, more in (
+                (go_up, c - t, c - t >= 0, c < n - 1),
+                (go_down, c + t, c + t < n, c > 0),
             ):
-                launch(copy, cond)
+                pl.when(cond)(arrived(block, hs, piece).wait_recv)
+                launch(go(hblk(block, hs, piece), block, piece), cond & more)
+                spread(hblk(block, hs, piece), block, piece, cond)
 
     def x_step(t):
-        pass_x(c - t, c - t >= 0)
-        pass_x(c + t, c + t < n)
+        for piece in range(PIECES):
+            pass_x(c - t, c - t >= 0, piece)
+            pass_x(c + t, c + t < n, piece)
 
     def w_step(t):
         pass_w(c - t, c - t >= 0)
@@ -433,10 +424,11 @@
 
         lax.fori_loop(0, tokens // LANES, one, 0)
 
-    hidden_step(1)
     send_w(1, 1)
     send_w(1, -1)
-    pass_x(c, None)
+    hidden_step(1)
+    for piece in range(PIECES):
+        pass_x(c, None, piece)
     for t in range(2, n):
         hidden_step(t)
         if t == 2:
@@ -459,6 +451,7 @@
         if t == 2:
             tables()
     x_step(n - 1)
+    w_step(n - 1)
     for block in range(n):
         for column in range(wide):
             mine = (column // subs == h) & (column % subs == s)
@@ -466,7 +459,8 @@
 
             @pl.when(jnp.logical_not(mine | across))
             def _():
-                arrived(block, column).wait_recv()
+                for piece in range(PIECES):
+                    arrived(block, column, piece).wait_recv()
 
     for number, copy in enumerate(locals_):
         if number != 2:
@@ -494,7 +488,6 @@
 
     lax.fori_loop(0, n, gather_low, 0)
     multiply(c, True)
-    w_step(n - 1)
     for t in range(1, n):
         for block, cond in ((c - t, c - t >= 0), (c + t, c + t < n)):
 
@@ -587,13 +580,6 @@
     gbsend[0:8, :] = (2.0 * t_dot(low, dq))[0:8]
     gbsend[8:16, :] = (2.0 * t_dot(low, dv))[8:16]
     for slot, target, cond in routes():
-        launch(
-            remote(
-                obuf.at[part(target, rows), :], outbuf.at[c], out_send.at[slot], out_recv.at[c], {"ctx": target}
-            ),
-            cond,
-        )
-    for slot, target, cond in routes():
         launch(remote(gbsend, gbrecv.at[c], gb_send.at[slot], gb_recv.at[c], {"ctx": target}), cond)
     out_ref[:, cols(c, LANES)] = obuf[part(c, rows), :]
     gbq_ref[:, cols(c, LANES)] = gbsend[0:8, :]
@@ -611,6 +597,13 @@
     for k in range(1, members):
         to = lax.rem(me + k, members)
         launch(remote(total, agbuf.at[me], ag_send.at[k], ag_recv.at[me], member(to)))
+    for slot, target, cond in routes():
+        launch(
+            remote(
+                obuf.at[part(target, rows), :], outbuf.at[c], out_send.at[slot], out_recv.at[c], {"ctx": target}
+            ),
+            cond,
+        )
     for k in range(1, members):
         frm = lax.rem(me + k, members)
         remote(total, agbuf.at[frm], ag_send.at[0], ag_recv.at[frm], {"sub": 1 - s}).wait_recv()
@@ -701,10 +694,10 @@
             vmem((8, LANES), f32),
             vmem((members, 8, LANES), f32),
             dma((6,)),
-            dma((2, n)),
-            dma((n,)),
-            dma((2, n)),
-            dma((n, wide)),
+            dma((2, n, PIECES)),
+            dma((n, PIECES)),
+            dma((2, n, PIECES)),
+            dma((n, wide, PIECES)),
             dma((2 * n, 3)),
             dma((n, 3)),
             dma((n, 3, 2)),
@@ -744,6 +737,7 @@
         and HEAD_DIM == LANES
         and a_query.shape[1] == 8
         and rows % LANES == 0
+        and rows % (16 * PIECES) == 0
         and rows // LANES <= 8
         and 2 * rows * n // LANES == members
         and rows * n * a_query.shape[0] <= 2**22

time: 122 us -> 111 us (0.910)
  Pallas kernels: 117 us -> 106 us
    pallas_call x1, Pallas kernels: 117 us -> 106 us  [one_head(): pl.pallas_call(functools.partial(one_head_kernel, n, subs, wide), out_sha...]
where the time goes in v3:
time: 111 us
  Pallas kernels  106 us (95%)
  local copies, waits for them, and re-layouts  4.35 us (4%)
    pallas_call x1, Pallas kernels, one_head(): pl.pallas_call(functools.partial(one_head_kernel, n, subs, wide), out_sha...  106 us
    unnamed x13, local copies, waits for them, and re-layouts  4.35 us

profile of v3, /device:TPU:0, one launch (start us, length us, event | category | flops | bytes accessed | tf_op | source)
XLA Modules:
  0.0 110.8 jit_solution(4691349502195321777)
XLA Ops:
  0.6 105.8 %shard_map.137 = (bf16[256,512]{1,0:T(8,128)(2,1)}, f32[8,4096]{1,0:T(8,128)}, f32[8,512]{1,0:T(8,128)}, f32[8,4096]{1,0:T(8,128)}, f32[8,512]{1,0:T(8,128)}) custom-call(bf16[256,1024]{1,0:T(8,128)(2,1)} %hid_ref.1, bf16[1024,512]{1,0:T(8,128)(2,1)} %wq_ref.1, bf16[1024,512]{1,0:T(8,128)(2,1)} %wk_ref.1, bf16[1024,512]{1,0:T(8,128)(2,1)} %wv_ref.1, ...), custom_call_target="tpu_custom_call" | custom-call | tf_op jit(solution)/shard_map/pallas_call | solution.py:663
  106.5 0.0 copy-start.1
  106.5 1.7 %copy.20 = bf16[256,512]{1,0:T(8,128)(2,1)} copy(bf16[256,512]{1,0:T(8,128)(2,1)} %get-tuple-element.20) | data formatting | bytes 524288
  108.2 0.0 copy-done.1
  108.2 0.0 copy-start.3
  108.2 0.0 copy-start
  108.2 0.7 copy.21
  108.8 0.1 copy-done.3
  108.9 0.6 copy.22
  109.5 0.0 copy-done
  109.5 0.0 copy-start.2
  109.5 0.7 copy.23
  110.2 0.1 copy-done.2
  110.2 0.6 copy.24
Async XLA Ops:
  106.5 1.7 %copy-start.1 = (f32[8,4096]{1,0:T(8,128)S(1)}, f32[8,4096]{1,0:T(8,128)}, u32[]{:S(2)}) copy-start(f32[8,4096]{1,0:T(8,128)} %get-tuple-element.11) | copy-start | bytes 393220
  108.2 0.7 copy-start.3
  108.2 1.3 %copy-start = (f32[8,4096]{1,0:T(8,128)S(1)}, f32[8,4096]{1,0:T(8,128)}, u32[]{:S(2)}) copy-start(f32[8,4096]{1,0:T(8,128)} %get-tuple-element.13) | copy-start | bytes 393220
  109.5 0.7 copy-start.2
